TPU v7x, 32 devices: a whole 2x2x4 slice. The times are simulated.
32 devices in a mesh: snap: 2 (over y), row: 4 (over z), col: 4 (over x, core).
Axes of the slice: x: 2, y: 2, z: 4, core: 2. Of those that a mesh axis runs over, the one named last changes fastest.
Arguments:
- orbitals: float32 [12288, 768], P(('snap', 'row', 'col')), parts along dimension 0, may hold values from -6 to 6
- screened: float32 [6, 6144, 6144], P('snap', 'row', 'col'), parts along dimension 0, may hold values from -0.0029296875 to 0.0029296875
- green_weight: float32 [6, 768], P('snap'), parts along dimension 0, may hold values from 0.05 to 1
- time_weight: float32 [3], replicated, may hold values from 0.3 to 1
Outputs:
- updated: float32 [12288, 768], P(('snap', 'row', 'col')), parts along dimension 0
There are 2 independent parts, one for each index of `snap`. A program takes and returns all parts, laid end to end along the dimension named above; an argument that names none is the same for every part. Nothing has to cross between parts.
All inputs are finite; a program needn't handle non-finite values.
Results may differ from a plain program's by a relative error of at most 0.00013.
Values sent between devices are 32-bit elements; how exact they have to be, the bound alone decides.
A program may use at most 128 MiB of HBM per device.

v0:
```python
import jax
import jax.numpy as jnp
from jax import lax
from jax.sharding import PartitionSpec as P

TIMES = 3
PASSES = 2


def from_root(block, axis, owner):
    block = jnp.where(lax.axis_index(axis) == owner, block, jnp.zeros_like(block))
    return lax.psum(block, axis)


def gather_rows(shard):
    return lax.all_gather(shard, "col", axis=0, tiled=True)


def scatter_rows(partial_value):
    return lax.psum_scatter(partial_value, "col", scatter_dimension=0, tiled=True)


def body(orbitals, screened, green_weight, time_weight):
    n_row = lax.axis_size("row")
    n_col = lax.axis_size("col")
    factor = n_col // n_row
    col_width = screened.shape[2]
    col_index = lax.axis_index("col")
    root = col_index // factor
    offset = col_index % factor * col_width
    own = orbitals
    rows = gather_rows(own)
    for step in range(PASSES):
        piece = lax.dynamic_slice_in_dim(rows, offset, col_width, 0)
        columns = from_root(piece, "row", root)
        partial_value = jnp.zeros(rows.shape, jnp.float32)
        for t in range(TIMES):
            green = lax.dot_general(
                rows * green_weight[t],
                columns,
                (((1,), (1,)), ((), ())),
                precision=lax.Precision.HIGHEST,
                preferred_element_type=jnp.float32,
            )
            applied = jnp.dot(
                green * screened[t],
                columns,
                precision=lax.Precision.HIGHEST,
                preferred_element_type=jnp.float32,
            )
            partial_value = partial_value + time_weight[t] * applied
        final = step == PASSES - 1
        own = own - scatter_rows(partial_value)
        if not final:
            rows = gather_rows(own)
    return own


def solution(mesh):
    in_specs = (P(("snap", "row", "col"), None), P("snap", "row", "col"), P("snap", None), P())
    out_specs = P(("snap", "row", "col"), None)
    return jax.shard_map(body, mesh=mesh, in_specs=in_specs, out_specs=out_specs, check_vma=False)
```

profile of v0, /device:TPU:0, one launch (start us, length us, event | category | flops | bytes accessed | tf_op | source)
XLA Modules:
  0.0 877.8 jit_solution(2341078948588468849)
XLA Ops:
  6.5 0.0 all-gather.3.cloned.1.call-start
  6.5 0.7 all-gather.3.cloned.1.call-update
  7.3 0.0 all-reduce.3.cloned.1.call-start
  7.3 41.8 %all-gather.3.cloned.1.call-done = f32[1536,768]{1,0:T(8,128)} async-done(((f32[384,768]{1,0:T(8,128)}), f32[1536,768]{1,0:T(8,128)}) %all-gather.3.cloned.1.call-update) | async-done | bytes 4718608 | tf_op jit(solution)/shard_map/all_gather | solution.py:16
  49.1 4.8 broadcast_select_fusion.1
  53.9 0.0 all-reduce.3.cloned.1.call-update
  53.9 0.0 reduce-scatter.3.cloned.1.call-start
  53.9 0.6 copy-done.4
  54.5 0.6 fusion.12
  55.2 0.0 copy-done.3
  55.2 170.7 %all-reduce.3.cloned.1.call-done = f32[1536,768]{1,0:T(8,128)} async-done(((f32[1536,768]{1,0:T(8,128)}), f32[1536,768]{1,0:T(8,128)}) %all-reduce.3.cloned.1.call-update) | async-done | bytes 4718608 | tf_op jit(solution)/shard_map/psum | solution.py:12
  225.9 28.3 %convolution_multiply_fusion.4 = f32[1536,1536]{1,0:T(8,128)} fusion(f32[1536,768]{1,0:T(8,128)} %all-reduce.3.cloned.1.call-done, f32[3,1536,1536]{2,1,0:T(8,128)} %param.5, f32[1536,768]{1,0:T(8,128)} %all-gather.3.cloned.1.call-done, f32[768]{0:T(1024)S(1)} %get-tuple-element.7), kind=kOutput, calls=%fused_computation.4 | convolution fusion | flops 21746810880 | bytes 28314624 | tf_op jit(solution)/shard_map/dot_general | solution.py:38
  254.2 28.0 %fusion.14 = f32[1536,768]{1,0:T(8,128)} fusion(f32[1536,1536]{1,0:T(8,128)} %convolution_multiply_fusion.4, f32[1536,768]{1,0:T(8,128)} %all-reduce.3.cloned.1.call-done), kind=kOutput, calls=%fused_computation.27 | convolution fusion | flops 21743271936 | bytes 18874368 | tf_op jit(solution)/shard_map/dot_general | solution.py:45
  282.2 0.0 slice-done.7
  282.2 0.0 slice-done
  282.2 0.0 slice-done.1
  282.2 0.0 slice-done.2
  282.2 0.0 slice-done.3
  282.2 0.0 slice-done.8
  282.2 0.0 slice-done.4
  282.2 26.8 %convolution_multiply_fusion.5 = f32[1536,1536]{1,0:T(8,128)} fusion(f32[1536,768]{1,0:T(8,128)} %all-reduce.3.cloned.1.call-done, f32[3,1536,1536]{2,1,0:T(8,128)S(1)} %bitcast.31, f32[1536,768]{1,0:T(8,128)S(1)} %bitcast.33, f32[768]{0:T(1024)S(1)} %get-tuple-element.6), kind=kOutput, calls=%fused_computation.5 | convolution fusion | flops 21746810880 | bytes 28314624 | tf_op jit(solution)/shard_map/dot_general | solution.py:38
  309.0 27.7 %fusion.13 = f32[1536,768]{1,0:T(8,128)} fusion(f32[1536,1536]{1,0:T(8,128)} %convolution_multiply_fusion.5, f32[1536,768]{1,0:T(8,128)} %all-reduce.3.cloned.1.call-done), kind=kOutput, calls=%fused_computation.26 | convolution fusion | flops 21743271936 | bytes 18874368 | tf_op jit(solution)/shard_map/dot_general | solution.py:45
  336.8 27.0 %convolution_multiply_fusion.3 = f32[1536,1536]{1,0:T(8,128)} fusion(f32[1536,768]{1,0:T(8,128)} %all-reduce.3.cloned.1.call-done, f32[3,1536,1536]{2,1,0:T(8,128)S(1)} %bitcast.31, f32[1536,768]{1,0:T(8,128)S(1)} %bitcast.33, f32[768]{0:T(1024)S(1)} %get-tuple-element.5), kind=kOutput, calls=%fused_computation.3 | convolution fusion | flops 21746810880 | bytes 28314624 | tf_op jit(solution)/shard_map/dot_general | solution.py:38
  363.8 31.6 %multiply_add_fusion.1 = f32[1536,768]{1,0:T(8,128)} fusion(f32[1536,768]{1,0:T(8,128)} %fusion.14, f32[1536,768]{1,0:T(8,128)} %fusion.13, f32[1536,1536]{1,0:T(8,128)} %convolution_multiply_fusion.3, f32[1536,768]{1,0:T(8,128)} %all-reduce.3.cloned.1.call-done, f32[]{:T(128)} %bitcast.4, f32[]{:T(128)} %bitcast.2, f32[]{:T(128)} %bitcast), kind=kOutput, calls=%fused_computation.10 | convolution fusion | flops 21749170176 | bytes 28311564 | tf_op jit(solution)/shard_map/dot_general | solution.py:45
  395.4 0.0 copy-start.2
  395.4 0.0 reduce-scatter.3.cloned.1.call-update
  395.4 0.0 all-gather.5.cloned.1.call-start
  395.5 47.0 %reduce-scatter.3.cloned.1.call-done = f32[384,768]{1,0:T(8,128)} async-done(((f32[1536,768]{1,0:T(8,128)}), f32[384,768]{1,0:T(8,128)}) %reduce-scatter.3.cloned.1.call-update) | async-done | bytes 1179664 | tf_op jit(solution)/shard_map/reduce_scatter | solution.py:20
  442.5 2.4 sub.8
  444.9 0.0 all-gather.5.cloned.1.call-update
  445.0 0.0 all-reduce.5.cloned.1.call-start
  445.0 37.5 %all-gather.5.cloned.1.call-done = f32[1536,768]{1,0:T(8,128)} async-done(((f32[384,768]{1,0:T(8,128)}), f32[1536,768]{1,0:T(8,128)}) %all-gather.5.cloned.1.call-update) | async-done | bytes 4718608 | tf_op jit(solution)/shard_map/all_gather | solution.py:16
  482.5 4.8 broadcast_select_fusion
  487.4 0.0 all-reduce.5.cloned.1.call-update
  487.4 0.0 reduce-scatter.5.cloned.1.call-start
  487.5 171.9 %all-reduce.5.cloned.1.call-done = f32[1536,768]{1,0:T(8,128)} async-done(((f32[1536,768]{1,0:T(8,128)}), f32[1536,768]{1,0:T(8,128)}) %all-reduce.5.cloned.1.call-update) | async-done | bytes 4718608 | tf_op jit(solution)/shard_map/psum | solution.py:12
  659.4 27.4 %convolution_multiply_fusion.1 = f32[1536,1536]{1,0:T(8,128)S(1)} fusion(f32[1536,768]{1,0:T(8,128)} %all-reduce.5.cloned.1.call-done, f32[3,1536,1536]{2,1,0:T(8,128)} %param.5, f32[1536,768]{1,0:T(8,128)} %all-gather.5.cloned.1.call-done, f32[768]{0:T(1024)S(1)} %get-tuple-element.7), kind=kOutput, calls=%fused_computation.1 | convolution fusion | flops 21746810880 | bytes 28314624 | tf_op jit(solution)/shard_map/dot_general | solution.py:38
  686.8 0.0 copy-done
  686.8 0.0 slice-start.10
  686.8 27.3 %convolution_multiply_fusion.2 = f32[1536,1536]{1,0:T(8,128)} fusion(f32[1536,768]{1,0:T(8,128)S(1)} %copy-done, f32[3,1536,1536]{2,1,0:T(8,128)} %param.5, f32[1536,768]{1,0:T(8,128)} %all-gather.5.cloned.1.call-done, f32[768]{0:T(1024)S(1)} %get-tuple-element.6), kind=kOutput, calls=%fused_computation.2 | convolution fusion | flops 21746810880 | bytes 28314624 | tf_op jit(solution)/shard_map/dot_general | solution.py:38
  714.1 0.0 slice-done.10
  714.2 28.4 %convolution_multiply_fusion = f32[1536,1536]{1,0:T(8,128)S(1)} fusion(f32[1536,768]{1,0:T(8,128)S(1)} %copy-done, f32[3,1536,1536]{2,1,0:T(8,128)} %param.5, f32[1536,768]{1,0:T(8,128)S(1)} %bitcast.35, f32[768]{0:T(1024)S(1)} %get-tuple-element.5), kind=kOutput, calls=%fused_computation | convolution fusion | flops 21746810880 | bytes 28314624 | tf_op jit(solution)/shard_map/dot_general | solution.py:38
  742.6 23.3 %fusion.16 = f32[1536,768]{1,0:T(8,128)S(1)} fusion(f32[1536,1536]{1,0:T(8,128)S(1)} %convolution_multiply_fusion.1, f32[1536,768]{1,0:T(8,128)S(1)} %copy-done), kind=kOutput, calls=%fused_computation.29 | convolution fusion | flops 21743271936 | bytes 18874368 | tf_op jit(solution)/shard_map/dot_general | solution.py:45
  765.9 28.4 %fusion.15 = f32[1536,768]{1,0:T(8,128)S(1)} fusion(f32[1536,1536]{1,0:T(8,128)} %convolution_multiply_fusion.2, f32[1536,768]{1,0:T(8,128)S(1)} %copy-done), kind=kOutput, calls=%fused_computation.28 | convolution fusion | flops 21743271936 | bytes 18874368 | tf_op jit(solution)/shard_map/dot_general | solution.py:45
  794.2 27.0 %multiply_add_fusion = f32[1536,768]{1,0:T(8,128)} fusion(f32[1536,768]{1,0:T(8,128)S(1)} %fusion.16, f32[1536,768]{1,0:T(8,128)S(1)} %fusion.15, f32[1536,1536]{1,0:T(8,128)S(1)} %convolution_multiply_fusion, f32[1536,768]{1,0:T(8,128)S(1)} %copy-done, f32[]{:T(128)} %bitcast.4, f32[]{:T(128)} %bitcast.2, f32[]{:T(128)} %bitcast), kind=kOutput, calls=%fused_computation.6 | convolution fusion | flops 21749170176 | bytes 28311564 | tf_op jit(solution)/shard_map/dot_general | solution.py:45
  821.2 0.0 reduce-scatter.5.cloned.1.call-update
  821.2 47.1 %reduce-scatter.5.cloned.1.call-done = f32[384,768]{1,0:T(8,128)} async-done(((f32[1536,768]{1,0:T(8,128)}), f32[384,768]{1,0:T(8,128)}) %reduce-scatter.5.cloned.1.call-update) | async-done | bytes 1179664 | tf_op jit(solution)/shard_map/reduce_scatter | solution.py:20
  868.3 2.4 sub.9
  (23 shorter events, 0.1 us)
Async XLA Ops:
  6.5 42.5 %all-gather.3.cloned.1.call-start = ((), (), s32[]{:S(2)}) async-start(), calls=%async_computation.2 | async-start | bytes 5898240 | tf_op jit(solution)/shard_map/all_gather | solution.py:16
  7.3 218.6 %all-reduce.3.cloned.1.call-start = ((), (), s32[]{:S(2)}) async-start(), calls=%async_computation.3 | async-start | bytes 9437184 | tf_op jit(solution)/shard_map/psum | solution.py:12
  53.9 0.7 copy-start.4
  53.9 1.3 copy-start.3
  53.9 228.3 %slice-start.7 = ((s8[4718592]{0:T(1024)(128)(4,1)}), s8[524288]{0:T(1024)(128)(4,1)S(1)}, s32[]{:S(2)}) async-start(s8[4718592]{0:T(1024)(128)(4,1)} %bitcast.32), calls=%async_computation.15 | async-start | bytes 1048576
  53.9 388.6 %reduce-scatter.3.cloned.1.call-start = ((), (), s32[]{:S(2)}) async-start(), calls=%async_computation.4 | async-start | bytes 5898240 | tf_op jit(solution)/shard_map/reduce_scatter | solution.py:20
  225.9 56.3 %slice-start = ((s8[28311552]{0:T(1024)(128)(4,1)}), s8[4194304]{0:T(1024)(128)(4,1)S(1)}, s32[]{:S(2)}) async-start(s8[28311552]{0:T(1024)(128)(4,1)} %bitcast.30), calls=%async_computation.8 | async-start | bytes 8388608
  225.9 56.3 %slice-start.1 = ((s8[28311552]{0:T(1024)(128)(4,1)}), s8[4194304]{0:T(1024)(128)(4,1)S(1)}, s32[]{:S(2)}) async-start(s8[28311552]{0:T(1024)(128)(4,1)} %bitcast.30), calls=%async_computation.9 | async-start | bytes 8388608
  225.9 56.3 %slice-start.2 = ((s8[28311552]{0:T(1024)(128)(4,1)}), s8[4194304]{0:T(1024)(128)(4,1)S(1)}, s32[]{:S(2)}) async-start(s8[28311552]{0:T(1024)(128)(4,1)} %bitcast.30), calls=%async_computation.10 | async-start | bytes 8388608
  225.9 56.3 %slice-start.3 = ((s8[28311552]{0:T(1024)(128)(4,1)}), s8[4194304]{0:T(1024)(128)(4,1)S(1)}, s32[]{:S(2)}) async-start(s8[28311552]{0:T(1024)(128)(4,1)} %bitcast.30), calls=%async_computation.11 | async-start | bytes 8388608
  225.9 56.3 %slice-start.8 = ((s8[4718592]{0:T(1024)(128)(4,1)}), s8[4194304]{0:T(1024)(128)(4,1)S(1)}, s32[]{:S(2)}) async-start(s8[4718592]{0:T(1024)(128)(4,1)} %bitcast.32), calls=%async_computation.16 | async-start | bytes 8388608
  254.1 28.0 %slice-start.4 = ((s8[28311552]{0:T(1024)(128)(4,1)}), s8[4194304]{0:T(1024)(128)(4,1)S(1)}, s32[]{:S(2)}) async-start(s8[28311552]{0:T(1024)(128)(4,1)} %bitcast.30), calls=%async_computation.12 | async-start | bytes 8388608
  254.1 28.1 %slice-start.5 = ((s8[28311552]{0:T(1024)(128)(4,1)}), s8[4194304]{0:T(1024)(128)(4,1)S(1)}, s32[]{:S(2)}) async-start(s8[28311552]{0:T(1024)(128)(4,1)} %bitcast.30), calls=%async_computation.13 | async-start | bytes 8388608
  254.2 28.1 %slice-start.6 = ((s8[28311552]{0:T(1024)(128)(4,1)}), s8[3145728]{0:T(1024)(128)(4,1)S(1)}, s32[]{:S(2)}) async-start(s8[28311552]{0:T(1024)(128)(4,1)} %bitcast.30), calls=%async_computation.14 | async-start | bytes 6291456
  395.4 47.1 %copy-start.2 = (f32[384,768]{1,0:T(8,128)S(1)}, f32[384,768]{1,0:T(8,128)}, u32[]{:S(2)}) copy-start(f32[384,768]{1,0:T(8,128)} %param.4) | copy-start | bytes 3538948
  395.4 87.1 %all-gather.5.cloned.1.call-start = ((), (), s32[]{:S(2)}) async-start(), calls=%async_computation.5 | async-start | bytes 5898240 | tf_op jit(solution)/shard_map/all_gather | solution.py:16
  445.0 214.4 %all-reduce.5.cloned.1.call-start = ((), (), s32[]{:S(2)}) async-start(), calls=%async_computation.6 | async-start | bytes 9437184 | tf_op jit(solution)/shard_map/psum | solution.py:12
  487.4 380.9 %reduce-scatter.5.cloned.1.call-start = ((), (), s32[]{:S(2)}) async-start(), calls=%async_computation.7 | async-start | bytes 5898240 | tf_op jit(solution)/shard_map/reduce_scatter | solution.py:20
  659.4 27.4 %copy-start = (f32[1536,768]{1,0:T(8,128)S(1)}, f32[1536,768]{1,0:T(8,128)}, u32[]{:S(2)}) copy-start(f32[1536,768]{1,0:T(8,128)} %all-reduce.5.cloned.1.call-done) | copy-start | bytes 14155780
  659.4 54.8 %slice-start.9 = ((s8[4718592]{0:T(1024)(128)(4,1)}), s8[4194304]{0:T(1024)(128)(4,1)S(1)}, s32[]{:S(2)}) async-start(s8[4718592]{0:T(1024)(128)(4,1)} %bitcast.34), calls=%async_computation.17 | async-start | bytes 8388608
  686.8 27.3 %slice-start.10 = ((s8[4718592]{0:T(1024)(128)(4,1)}), s8[524288]{0:T(1024)(128)(4,1)S(1)}, s32[]{:S(2)}) async-start(s8[4718592]{0:T(1024)(128)(4,1)} %bitcast.34), calls=%async_computation.18 | async-start | bytes 1048576
  821.2 47.1 %copy-start.1 = (f32[384,768]{1,0:T(8,128)S(1)}, f32[384,768]{1,0:T(8,128)}, u32[]{:S(2)}) copy-start(f32[384,768]{1,0:T(8,128)} %sub.8) | copy-start | bytes 3538948
Sparse Core Ops, SparseCore 0:
  8.9 40.1 all-gather.2
  54.0 171.8 all-reduce.2
  395.5 46.9 reduce-scatter.2
  445.1 37.4 all-gather.4
  487.5 171.8 all-reduce.4
  821.4 46.9 reduce-scatter.4
where the time goes:
time: 886 us; the launch traced here: 878 us
  waiting for transfers between devices  517 us (58%)
  matrix products  331 us (37%)
  other arithmetic  14.5 us (2%)
  between operations  13.9 us (2%)
    psum x2, waiting for transfers between devices, from_root(): return lax.psum(block, axis)  343 us
    dot_general x6, matrix products, body(): jnp.dot(green * screened[t], columns, precision=lax.Precision.HIGHEST, pr...  166 us
    dot_general x6, matrix products, body(): lax.dot_general(rows * green_weight[t], columns, (((1,), (1,)), ((), ()))...  165 us
    reduce_scatter x2, waiting for transfers between devices, scatter_rows(): lax.psum_scatter(partial_value, 'col', scatter_dimension=0, tiled=True)  94.1 us
    all_gather x2, waiting for transfers between devices, gather_rows(): return lax.all_gather(shard, 'col', axis=0, tiled=True)  79.3 us
  transfers between devices with their start and end apart: 6, of which 6 were waited for; matrix products, arithmetic and copies ran while one was open for 0% of the time, Pallas kernels for 0%

commit v1 on v0

--- a/solution.py
+++ b/solution.py
@@ -9,7 +9,7 @@
 
 def from_root(block, axis, owner):
     block = jnp.where(lax.axis_index(axis) == owner, block, jnp.zeros_like(block))
-    return lax.psum(block, axis)
+    return jnp.sum(lax.all_gather(block, axis), axis=0)
 
 
 def gather_rows(shard):

time: 886 us -> 1210 us (1.37)
  waiting for transfers between devices: 517 us -> 818 us
  other arithmetic: 14.5 us -> 35.2 us
    all_gather x0 -> x2, waiting for transfers between devices: none -> 644 us  [from_root(): return jnp.sum(lax.all_gather(block, axis), axis=0)]
    psum x2 -> x0, waiting for transfers between devices: 343 us -> none  [from_root(): return lax.psum(block, axis)]
    reduce_sum x0 -> x2, other arithmetic: none -> 20.8 us  [from_root(): return jnp.sum(lax.all_gather(block, axis), axis=0)]
where the time goes in v1:
time: 1210 us
  waiting for transfers between devices  818 us (68%)
  matrix products  339 us (28%)
  other arithmetic  35.2 us (3%)
  between operations  13.9 us (1%)
    all_gather x2, waiting for transfers between devices, from_root(): return jnp.sum(lax.all_gather(block, axis), axis=0)  644 us
    dot_general x6, matrix products, body(): jnp.dot(green * screened[t], columns, precision=lax.Precision.HIGHEST, pr...  175 us
    dot_general x6, matrix products, body(): lax.dot_general(rows * green_weight[t], columns, (((1,), (1,)), ((), ()))...  164 us
    reduce_scatter x2, waiting for transfers between devices, scatter_rows(): lax.psum_scatter(partial_value, 'col', scatter_dimension=0, tiled=True)  93.9 us
    all_gather x2, waiting for transfers between devices, gather_rows(): return lax.all_gather(shard, 'col', axis=0, tiled=True)  79.3 us
  transfers between devices with their start and end apart: 6, of which 6 were waited for; matrix products, arithmetic and copies ran while one was open for 0% of the time, Pallas kernels for 0%

profile of v1, /device:TPU:0, one launch (start us, length us, event | category | flops | bytes accessed | tf_op | source)
XLA Modules:
  0.0 1207.3 jit_solution(12461725232774533941)
XLA Ops:
  6.5 0.7 all-gather.7.cloned.1.call-update
  7.3 0.0 all-gather.11.cloned.1.call-start
  7.3 41.8 %all-gather.7.cloned.1.call-done = f32[1536,768]{1,0:T(8,128)} async-done(((f32[384,768]{1,0:T(8,128)}), f32[1536,768]{1,0:T(8,128)}) %all-gather.7.cloned.1.call-update) | async-done | bytes 4718608 | tf_op jit(solution)/shard_map/all_gather | solution.py:16
  49.1 4.8 broadcast_select_fusion.1
  53.9 0.0 all-gather.11.cloned.1.call-update
  53.9 0.0 reduce-scatter.3.cloned.1.call-start
  54.0 0.6 copy-done.3
  54.5 0.7 fusion.12
  55.2 0.0 copy-done.2
  55.3 321.3 %all-gather.11.cloned.1.call-done = f32[6144,768]{1,0:T(8,128)} async-done(((f32[1536,768]{1,0:T(8,128)}), f32[6144,768]{1,0:T(8,128)}) %all-gather.11.cloned.1.call-update) | async-done | bytes 18874384 | tf_op jit(solution)/shard_map/all_gather | solution.py:12
  376.5 10.4 reduce_sum.18
  386.9 28.4 %convolution_multiply_fusion.4 = f32[1536,1536]{1,0:T(8,128)} fusion(f32[1536,768]{1,0:T(8,128)} %reduce_sum.18, f32[3,1536,1536]{2,1,0:T(8,128)} %param.5, f32[1536,768]{1,0:T(8,128)} %all-gather.7.cloned.1.call-done, f32[768]{0:T(1024)S(1)} %get-tuple-element.7), kind=kOutput, calls=%fused_computation.4 | convolution fusion | flops 21746810880 | bytes 28314624 | tf_op jit(solution)/shard_map/dot_general | solution.py:38
  415.4 28.0 %fusion.14 = f32[1536,768]{1,0:T(8,128)} fusion(f32[1536,1536]{1,0:T(8,128)} %convolution_multiply_fusion.4, f32[1536,768]{1,0:T(8,128)} %reduce_sum.18), kind=kOutput, calls=%fused_computation.27 | convolution fusion | flops 21743271936 | bytes 18874368 | tf_op jit(solution)/shard_map/dot_general | solution.py:45
  443.4 0.0 slice-done.1
  443.4 0.0 slice-done.2
  443.4 0.0 slice-done.3
  443.4 0.0 slice-done.15
  443.4 0.0 slice-done.4
  443.4 0.0 slice-done.5
  443.4 0.0 slice-done.6
  443.5 26.8 %convolution_multiply_fusion.5 = f32[1536,1536]{1,0:T(8,128)} fusion(f32[1536,768]{1,0:T(8,128)} %reduce_sum.18, f32[3,1536,1536]{2,1,0:T(8,128)S(1)} %bitcast.33, f32[1536,768]{1,0:T(8,128)S(1)} %bitcast.37, f32[768]{0:T(1024)S(1)} %get-tuple-element.6), kind=kOutput, calls=%fused_computation.5 | convolution fusion | flops 21746810880 | bytes 28314624 | tf_op jit(solution)/shard_map/dot_general | solution.py:38
  470.3 27.8 %fusion.13 = f32[1536,768]{1,0:T(8,128)} fusion(f32[1536,1536]{1,0:T(8,128)} %convolution_multiply_fusion.5, f32[1536,768]{1,0:T(8,128)} %reduce_sum.18), kind=kOutput, calls=%fused_computation.26 | convolution fusion | flops 21743271936 | bytes 18874368 | tf_op jit(solution)/shard_map/dot_general | solution.py:45
  498.0 27.0 %convolution_multiply_fusion.3 = f32[1536,1536]{1,0:T(8,128)} fusion(f32[1536,768]{1,0:T(8,128)} %reduce_sum.18, f32[3,1536,1536]{2,1,0:T(8,128)S(1)} %bitcast.33, f32[1536,768]{1,0:T(8,128)S(1)} %bitcast.37, f32[768]{0:T(1024)S(1)} %get-tuple-element.5), kind=kOutput, calls=%fused_computation.3 | convolution fusion | flops 21746810880 | bytes 28314624 | tf_op jit(solution)/shard_map/dot_general | solution.py:38
  525.0 31.6 %multiply_add_fusion.1 = f32[1536,768]{1,0:T(8,128)} fusion(f32[1536,768]{1,0:T(8,128)} %fusion.14, f32[1536,768]{1,0:T(8,128)} %fusion.13, f32[1536,1536]{1,0:T(8,128)} %convolution_multiply_fusion.3, f32[1536,768]{1,0:T(8,128)} %reduce_sum.18, f32[]{:T(128)} %bitcast.5, f32[]{:T(128)} %bitcast.3, f32[]{:T(128)} %bitcast), kind=kOutput, calls=%fused_computation.10 | convolution fusion | flops 21749170176 | bytes 28311564 | tf_op jit(solution)/shard_map/dot_general | solution.py:45
  556.7 0.0 copy-start.1
  556.7 0.0 reduce-scatter.3.cloned.1.call-update
  556.7 0.0 all-gather.9.cloned.1.call-start
  556.8 46.9 %reduce-scatter.3.cloned.1.call-done = f32[384,768]{1,0:T(8,128)} async-done(((f32[1536,768]{1,0:T(8,128)}), f32[384,768]{1,0:T(8,128)}) %reduce-scatter.3.cloned.1.call-update) | async-done | bytes 1179664 | tf_op jit(solution)/shard_map/reduce_scatter | solution.py:20
  603.7 0.0 copy-done.1
  603.7 2.4 sub.8
  606.1 0.0 all-gather.9.cloned.1.call-update
  606.2 0.0 all-gather.13.cloned.1.call-start
  606.2 37.5 %all-gather.9.cloned.1.call-done = f32[1536,768]{1,0:T(8,128)} async-done(((f32[384,768]{1,0:T(8,128)}), f32[1536,768]{1,0:T(8,128)}) %all-gather.9.cloned.1.call-update) | async-done | bytes 4718608 | tf_op jit(solution)/shard_map/all_gather | solution.py:16
  643.7 4.8 broadcast_select_fusion
  648.5 0.0 all-gather.13.cloned.1.call-update
  648.6 0.0 reduce-scatter.5.cloned.1.call-start
  648.6 322.6 %all-gather.13.cloned.1.call-done = f32[6144,768]{1,0:T(8,128)} async-done(((f32[1536,768]{1,0:T(8,128)}), f32[6144,768]{1,0:T(8,128)}) %all-gather.13.cloned.1.call-update) | async-done | bytes 18874384 | tf_op jit(solution)/shard_map/all_gather | solution.py:12
  971.2 10.4 reduce_sum.19
  981.6 28.2 %convolution_multiply_fusion.1 = f32[1536,1536]{1,0:T(8,128)} fusion(f32[1536,768]{1,0:T(8,128)} %reduce_sum.19, f32[3,1536,1536]{2,1,0:T(8,128)} %param.5, f32[1536,768]{1,0:T(8,128)} %all-gather.9.cloned.1.call-done, f32[768]{0:T(1024)S(1)} %get-tuple-element.7), kind=kOutput, calls=%fused_computation.1 | convolution fusion | flops 21746810880 | bytes 28314624 | tf_op jit(solution)/shard_map/dot_general | solution.py:38
  1009.8 27.9 %fusion.16 = f32[1536,768]{1,0:T(8,128)} fusion(f32[1536,1536]{1,0:T(8,128)} %convolution_multiply_fusion.1, f32[1536,768]{1,0:T(8,128)} %reduce_sum.19), kind=kOutput, calls=%fused_computation.29 | convolution fusion | flops 21743271936 | bytes 18874368 | tf_op jit(solution)/shard_map/dot_general | solution.py:45
  1037.8 0.0 slice-done.9
  1037.8 27.0 %convolution_multiply_fusion.2 = f32[1536,1536]{1,0:T(8,128)} fusion(f32[1536,768]{1,0:T(8,128)} %reduce_sum.19, f32[3,1536,1536]{2,1,0:T(8,128)S(1)} %bitcast.35, f32[1536,768]{1,0:T(8,128)S(1)} %bitcast.39, f32[768]{0:T(1024)S(1)} %get-tuple-element.6), kind=kOutput, calls=%fused_computation.2 | convolution fusion | flops 21746810880 | bytes 28314624 | tf_op jit(solution)/shard_map/dot_general | solution.py:38
  1064.8 27.8 %fusion.15 = f32[1536,768]{1,0:T(8,128)} fusion(f32[1536,1536]{1,0:T(8,128)} %convolution_multiply_fusion.2, f32[1536,768]{1,0:T(8,128)} %reduce_sum.19), kind=kOutput, calls=%fused_computation.28 | convolution fusion | flops 21743271936 | bytes 18874368 | tf_op jit(solution)/shard_map/dot_general | solution.py:45
  1092.7 26.7 %convolution_multiply_fusion = f32[1536,1536]{1,0:T(8,128)} fusion(f32[1536,768]{1,0:T(8,128)} %reduce_sum.19, f32[3,1536,1536]{2,1,0:T(8,128)S(1)} %bitcast.35, f32[1536,768]{1,0:T(8,128)S(1)} %bitcast.39, f32[768]{0:T(1024)S(1)} %get-tuple-element.5), kind=kOutput, calls=%fused_computation | convolution fusion | flops 21746810880 | bytes 28314624 | tf_op jit(solution)/shard_map/dot_general | solution.py:38
  1119.4 31.5 %multiply_add_fusion = f32[1536,768]{1,0:T(8,128)} fusion(f32[1536,768]{1,0:T(8,128)} %fusion.16, f32[1536,768]{1,0:T(8,128)} %fusion.15, f32[1536,1536]{1,0:T(8,128)} %convolution_multiply_fusion, f32[1536,768]{1,0:T(8,128)} %reduce_sum.19, f32[]{:T(128)} %bitcast.5, f32[]{:T(128)} %bitcast.3, f32[]{:T(128)} %bitcast), kind=kOutput, calls=%fused_computation.6 | convolution fusion | flops 21749170176 | bytes 28311564 | tf_op jit(solution)/shard_map/dot_general | solution.py:45
  1150.9 0.0 reduce-scatter.5.cloned.1.call-update
  1150.9 47.0 %reduce-scatter.5.cloned.1.call-done = f32[384,768]{1,0:T(8,128)} async-done(((f32[1536,768]{1,0:T(8,128)}), f32[384,768]{1,0:T(8,128)}) %reduce-scatter.5.cloned.1.call-update) | async-done | bytes 1179664 | tf_op jit(solution)/shard_map/reduce_scatter | solution.py:20
  1197.9 2.4 sub.9
  (38 shorter events, 0.1 us)
Async XLA Ops:
  6.5 42.5 %all-gather.7.cloned.1.call-start = ((), (), s32[]{:S(2)}) async-start(), calls=%async_computation.2 | async-start | bytes 5898240 | tf_op jit(solution)/shard_map/all_gather | solution.py:16
  7.3 369.3 %all-gather.11.cloned.1.call-start = ((), (), s32[]{:S(2)}) async-start(), calls=%async_computation.6 | async-start | bytes 23592960 | tf_op jit(solution)/shard_map/all_gather | solution.py:12
  53.9 0.7 copy-start.3
  53.9 1.3 copy-start.2
  53.9 549.8 %reduce-scatter.3.cloned.1.call-start = ((), (), s32[]{:S(2)}) async-start(), calls=%async_computation.3 | async-start | bytes 5898240 | tf_op jit(solution)/shard_map/reduce_scatter | solution.py:20
  376.5 66.8 %slice-start.14 = ((s8[4718592]{0:T(1024)(128)(4,1)}), s8[524288]{0:T(1024)(128)(4,1)S(1)}, s32[]{:S(2)}) async-start(s8[4718592]{0:T(1024)(128)(4,1)} %bitcast.36), calls=%async_computation.22 | async-start | bytes 1048576
  386.9 56.4 %slice-start = ((s8[28311552]{0:T(1024)(128)(4,1)}), s8[4194304]{0:T(1024)(128)(4,1)S(1)}, s32[]{:S(2)}) async-start(s8[28311552]{0:T(1024)(128)(4,1)} %bitcast.32), calls=%async_computation.8 | async-start | bytes 8388608
  386.9 56.4 %slice-start.1 = ((s8[28311552]{0:T(1024)(128)(4,1)}), s8[4194304]{0:T(1024)(128)(4,1)S(1)}, s32[]{:S(2)}) async-start(s8[28311552]{0:T(1024)(128)(4,1)} %bitcast.32), calls=%async_computation.9 | async-start | bytes 8388608
  386.9 56.4 %slice-start.2 = ((s8[28311552]{0:T(1024)(128)(4,1)}), s8[4194304]{0:T(1024)(128)(4,1)S(1)}, s32[]{:S(2)}) async-start(s8[28311552]{0:T(1024)(128)(4,1)} %bitcast.32), calls=%async_computation.10 | async-start | bytes 8388608
  386.9 56.5 %slice-start.3 = ((s8[28311552]{0:T(1024)(128)(4,1)}), s8[4194304]{0:T(1024)(128)(4,1)S(1)}, s32[]{:S(2)}) async-start(s8[28311552]{0:T(1024)(128)(4,1)} %bitcast.32), calls=%async_computation.11 | async-start | bytes 8388608
  386.9 56.5 %slice-start.15 = ((s8[4718592]{0:T(1024)(128)(4,1)}), s8[4194304]{0:T(1024)(128)(4,1)S(1)}, s32[]{:S(2)}) async-start(s8[4718592]{0:T(1024)(128)(4,1)} %bitcast.36), calls=%async_computation.23 | async-start | bytes 8388608
  415.3 28.1 %slice-start.4 = ((s8[28311552]{0:T(1024)(128)(4,1)}), s8[4194304]{0:T(1024)(128)(4,1)S(1)}, s32[]{:S(2)}) async-start(s8[28311552]{0:T(1024)(128)(4,1)} %bitcast.32), calls=%async_computation.12 | async-start | bytes 8388608
  415.3 28.1 %slice-start.5 = ((s8[28311552]{0:T(1024)(128)(4,1)}), s8[4194304]{0:T(1024)(128)(4,1)S(1)}, s32[]{:S(2)}) async-start(s8[28311552]{0:T(1024)(128)(4,1)} %bitcast.32), calls=%async_computation.13 | async-start | bytes 8388608
  415.4 28.1 %slice-start.6 = ((s8[28311552]{0:T(1024)(128)(4,1)}), s8[3145728]{0:T(1024)(128)(4,1)S(1)}, s32[]{:S(2)}) async-start(s8[28311552]{0:T(1024)(128)(4,1)} %bitcast.32), calls=%async_computation.14 | async-start | bytes 6291456
  556.7 47.0 %copy-start.1 = (f32[384,768]{1,0:T(8,128)S(1)}, f32[384,768]{1,0:T(8,128)}, u32[]{:S(2)}) copy-start(f32[384,768]{1,0:T(8,128)} %param.4) | copy-start | bytes 3538948
  556.7 87.0 %all-gather.9.cloned.1.call-start = ((), (), s32[]{:S(2)}) async-start(), calls=%async_computation.4 | async-start | bytes 5898240 | tf_op jit(solution)/shard_map/all_gather | solution.py:16
  606.2 365.0 %all-gather.13.cloned.1.call-start = ((), (), s32[]{:S(2)}) async-start(), calls=%async_computation.7 | async-start | bytes 23592960 | tf_op jit(solution)/shard_map/all_gather | solution.py:12
  648.6 549.3 %reduce-scatter.5.cloned.1.call-start = ((), (), s32[]{:S(2)}) async-start(), calls=%async_computation.5 | async-start | bytes 5898240 | tf_op jit(solution)/shard_map/reduce_scatter | solution.py:20
  971.2 66.6 %slice-start.16 = ((s8[4718592]{0:T(1024)(128)(4,1)}), s8[524288]{0:T(1024)(128)(4,1)S(1)}, s32[]{:S(2)}) async-start(s8[4718592]{0:T(1024)(128)(4,1)} %bitcast.38), calls=%async_computation.24 | async-start | bytes 1048576
  981.6 56.2 %slice-start.7 = ((s8[28311552]{0:T(1024)(128)(4,1)}), s8[4194304]{0:T(1024)(128)(4,1)S(1)}, s32[]{:S(2)}) async-start(s8[28311552]{0:T(1024)(128)(4,1)} %bitcast.34), calls=%async_computation.15 | async-start | bytes 8388608
  981.6 56.2 %slice-start.8 = ((s8[28311552]{0:T(1024)(128)(4,1)}), s8[4194304]{0:T(1024)(128)(4,1)S(1)}, s32[]{:S(2)}) async-start(s8[28311552]{0:T(1024)(128)(4,1)} %bitcast.34), calls=%async_computation.16 | async-start | bytes 8388608
  981.6 56.2 %slice-start.9 = ((s8[28311552]{0:T(1024)(128)(4,1)}), s8[4194304]{0:T(1024)(128)(4,1)S(1)}, s32[]{:S(2)}) async-start(s8[28311552]{0:T(1024)(128)(4,1)} %bitcast.34), calls=%async_computation.17 | async-start | bytes 8388608
  981.6 56.2 %slice-start.10 = ((s8[28311552]{0:T(1024)(128)(4,1)}), s8[4194304]{0:T(1024)(128)(4,1)S(1)}, s32[]{:S(2)}) async-start(s8[28311552]{0:T(1024)(128)(4,1)} %bitcast.34), calls=%async_computation.18 | async-start | bytes 8388608
  981.6 56.2 %slice-start.17 = ((s8[4718592]{0:T(1024)(128)(4,1)}), s8[4194304]{0:T(1024)(128)(4,1)S(1)}, s32[]{:S(2)}) async-start(s8[4718592]{0:T(1024)(128)(4,1)} %bitcast.38), calls=%async_computation.25 | async-start | bytes 8388608
  1009.8 28.0 %slice-start.11 = ((s8[28311552]{0:T(1024)(128)(4,1)}), s8[4194304]{0:T(1024)(128)(4,1)S(1)}, s32[]{:S(2)}) async-start(s8[28311552]{0:T(1024)(128)(4,1)} %bitcast.34), calls=%async_computation.19 | async-start | bytes 8388608
  1009.8 28.0 %slice-start.12 = ((s8[28311552]{0:T(1024)(128)(4,1)}), s8[4194304]{0:T(1024)(128)(4,1)S(1)}, s32[]{:S(2)}) async-start(s8[28311552]{0:T(1024)(128)(4,1)} %bitcast.34), calls=%async_computation.20 | async-start | bytes 8388608
  1009.8 28.0 %slice-start.13 = ((s8[28311552]{0:T(1024)(128)(4,1)}), s8[3145728]{0:T(1024)(128)(4,1)S(1)}, s32[]{:S(2)}) async-start(s8[28311552]{0:T(1024)(128)(4,1)} %bitcast.34), calls=%async_computation.21 | async-start | bytes 6291456
  1150.9 47.0 %copy-start = (f32[384,768]{1,0:T(8,128)S(1)}, f32[384,768]{1,0:T(8,128)}, u32[]{:S(2)}) copy-start(f32[384,768]{1,0:T(8,128)} %sub.8) | copy-start | bytes 3538948
Sparse Core Ops, SparseCore 0:
  8.9 40.1 all-gather.6
  54.0 322.4 all-gather.10
  556.9 46.8 reduce-scatter.2
  606.3 37.4 all-gather.8
  648.7 322.4 all-gather.12
  1151.0 46.8 reduce-scatter.4
